TPU v7x, 32 devices: a whole 2x2x4 slice. The times are simulated.
32 devices in a mesh: region: 8 (over y, x, core), tile: 4 (over z).
Axes of the slice: x: 2, y: 2, z: 4, core: 2. Of those that a mesh axis runs over, the one named last changes fastest.
Arguments:
- params: float32 [256, 59, 128], P(('region', 'tile')), may hold values from -6 to 6
- first_moment: float32 [256, 59, 128], P(('region', 'tile')), may hold values from -0.006 to 0.006
- second_moment: float32 [256, 59, 128], P(('region', 'tile')), may hold values from 1e-09 to 2e-05
- view_basis: float32 [16], replicated, may hold values from -1.5 to 1.5
- target: float32 [32, 3, 1024], P(('region', 'tile')), may hold values from 0 to 1
- tile_blocks: int32 [32, 4], P(('region', 'tile')), may hold values from 0 to 31, as said below
- moving: int32 [32, 4], P(('region', 'tile')), may hold values from 0 to 7, as said below
Outputs:
- new_params: float32 [256, 59, 128], P(('region', 'tile'))
- new_first: float32 [256, 59, 128], P(('region', 'tile'))
- new_second: float32 [256, 59, 128], P(('region', 'tile'))
- image: float32 [32, 3, 1024], P(('region', 'tile'))
Inputs may be any that keep to these rules, and one draw needn't show every extreme that they name: `tile_blocks`: row i lists the blocks of the tile of device i front to back, as ids within that device's region; it names exactly one block of each of the region's 4 devices, the device at tile index k owning ids k * 8 to (k + 1) * 8 - 1. `moving`: row i names 4 different blocks of device i, counted from 0 within the device.
All inputs are finite; a program needn't handle non-finite values.
Results may differ from a plain program's by a relative error of at most 0.0003.
Values sent between devices are 32-bit elements; how exact they have to be, the bound alone decides.
No kernel may reach another device: no remote copies, remote signals or barrier semaphores. Data moves between devices by JAX's collectives and lax.ppermute only.
A program may use at most 64 MiB of HBM per device.

v0:
```python
import jax
import jax.numpy as jnp
from jax import lax
from jax.sharding import PartitionSpec as P

SH = 16
TILE_SIDE = 32
PIX = 1024
beta_one = 0.9
beta_two = 0.999
adam_eps = 1e-08
adam_step = 10.0
highest = lax.Precision.HIGHEST


def shifted(shard, axis, by):
    peers = lax.axis_size(axis)
    return lax.ppermute(shard, axis, [(i, (i + by) % peers) for i in range(peers)])


def step_rates():
    return jnp.concatenate(
        [
            jnp.full((3,), 0.002, jnp.float32),
            jnp.full((3,), 0.005, jnp.float32),
            jnp.full((4,), 0.001, jnp.float32),
            jnp.full((1,), 0.05, jnp.float32),
            jnp.full((3 * SH,), 0.0025, jnp.float32),
        ]
    )


def project(values, view_basis):
    side = float(TILE_SIDE)
    mean_x = 0.5 * side + 0.375 * side * jnp.tanh(values[..., 0, :])
    mean_y = 0.5 * side + 0.375 * side * jnp.tanh(values[..., 1, :])
    zoom_factor = 3.0 / (1.0 + jax.nn.softplus(values[..., 2, :]))
    extent = side / 32.0 * 1.5 * jnp.exp(jnp.tanh(values[..., 3:6, :]))
    extent_sq = extent * extent
    rotation = values[..., 6:10, :]
    rot_norm = jnp.sqrt(jnp.sum(rotation * rotation, axis=-2, keepdims=True))
    rotation = rotation / jnp.maximum(rot_norm, 1.0)
    quat_w = rotation[..., 0, :]
    quat_x = rotation[..., 1, :]
    quat_y = rotation[..., 2, :]
    quat_z = rotation[..., 3, :]
    upper_row = [
        1.0 - 2.0 * (quat_y * quat_y + quat_z * quat_z),
        2.0 * (quat_x * quat_y - quat_w * quat_z),
        2.0 * (quat_x * quat_z + quat_w * quat_y),
    ]
    lower_row = [
        2.0 * (quat_x * quat_y + quat_w * quat_z),
        1.0 - 2.0 * (quat_x * quat_x + quat_z * quat_z),
        2.0 * (quat_y * quat_z - quat_w * quat_x),
    ]
    zoom_sq = zoom_factor * zoom_factor
    cov_xx = (
        zoom_sq
        * (
            upper_row[0] * upper_row[0] * extent_sq[..., 0, :]
            + upper_row[1] * upper_row[1] * extent_sq[..., 1, :]
            + upper_row[2] * upper_row[2] * extent_sq[..., 2, :]
        )
        + 0.3
    )
    cov_yy = (
        zoom_sq
        * (
            lower_row[0] * lower_row[0] * extent_sq[..., 0, :]
            + lower_row[1] * lower_row[1] * extent_sq[..., 1, :]
            + lower_row[2] * lower_row[2] * extent_sq[..., 2, :]
        )
        + 0.3
    )
    cov_xy = zoom_sq * (
        upper_row[0] * lower_row[0] * extent_sq[..., 0, :]
        + upper_row[1] * lower_row[1] * extent_sq[..., 1, :]
        + upper_row[2] * lower_row[2] * extent_sq[..., 2, :]
    )
    determinant = cov_xx * cov_yy - cov_xy * cov_xy
    opacity = 0.99 * jax.nn.sigmoid(values[..., 10, :] - 4.0)
    harmonics = values[..., 11:, :].reshape(values.shape[:-2] + (3, SH, values.shape[-1]))
    colours = jax.nn.sigmoid(
        jnp.einsum("...ckg,k->...cg", harmonics, view_basis, precision=highest)
    )
    return jnp.stack(
        [
            mean_x,
            mean_y,
            cov_yy / determinant,
            -cov_xy / determinant,
            cov_xx / determinant,
            opacity,
            colours[..., 0, :],
            colours[..., 1, :],
            colours[..., 2, :],
        ],
        axis=-2,
    )


def composite(splat_list, wanted):
    width = splat_list.shape[2]
    pixels = jnp.arange(PIX)
    centre_x = (pixels % TILE_SIDE).astype(jnp.float32) + 0.5
    centre_y = (pixels // TILE_SIDE).astype(jnp.float32) + 0.5
    strict = (jnp.arange(width)[:, None] < jnp.arange(width)[None, :]).astype(jnp.float32)
    inclusive_mask = (jnp.arange(width)[:, None] <= jnp.arange(width)[None, :]).astype(jnp.float32)

    def footprint(splats):
        offset_x = centre_x[:, None] - splats[0][None, :]
        offset_y = centre_y[:, None] - splats[1][None, :]
        exponent = -0.5 * (
            splats[2] * offset_x * offset_x
            + 2.0 * splats[3] * offset_x * offset_y
            + splats[4] * offset_y * offset_y
        )
        spread = jnp.exp(exponent)
        alphas = splats[5] * spread
        log_keep = jnp.log1p(-alphas)
        return (offset_x, offset_y, spread, alphas, log_keep)

    def forward(running, splats):
        log_trans, colour_sum = running
        offset_x, offset_y, spread, alphas, log_keep = footprint(splats)
        log_here = log_trans[:, None] + jnp.dot(log_keep, strict, precision=highest)
        weight = alphas * jnp.exp(log_here)
        colour_sum = colour_sum + jnp.dot(weight, splats[6:9].T, precision=highest)
        return ((log_trans + jnp.sum(log_keep, axis=1), colour_sum), None)

    initial = (jnp.zeros((PIX,), jnp.float32), jnp.zeros((PIX, 3), jnp.float32))
    (_, colour_sum), _ = lax.scan(forward, initial, splat_list)
    errors = 2.0 * (colour_sum - wanted.T)
    totals = jnp.sum(errors * colour_sum, axis=1)

    def backward(running, splats):
        log_trans, before = running
        offset_x, offset_y, spread, alphas, log_keep = footprint(splats)
        log_here = log_trans[:, None] + jnp.dot(log_keep, strict, precision=highest)
        trans = jnp.exp(log_here)
        weight = alphas * trans
        shading = jnp.dot(errors, splats[6:9], precision=highest)
        covered = before[:, None] + jnp.dot(weight * shading, inclusive_mask, precision=highest)
        d_alpha = trans * shading - (totals[:, None] - covered) / (1.0 - alphas)
        d_exponent = d_alpha * alphas
        d_colour = jnp.dot(errors.T, weight, precision=highest)
        gradient = jnp.stack(
            [
                jnp.sum(d_exponent * (splats[2] * offset_x + splats[3] * offset_y), axis=0),
                jnp.sum(d_exponent * (splats[3] * offset_x + splats[4] * offset_y), axis=0),
                jnp.sum(-0.5 * offset_x * offset_x * d_exponent, axis=0),
                jnp.sum(-offset_x * offset_y * d_exponent, axis=0),
                jnp.sum(-0.5 * offset_y * offset_y * d_exponent, axis=0),
                jnp.sum(d_alpha * spread, axis=0),
                d_colour[0],
                d_colour[1],
                d_colour[2],
            ]
        )
        return ((log_trans + jnp.sum(log_keep, axis=1), covered[:, -1]), gradient)

    _, splat_grads = lax.scan(
        backward, (jnp.zeros((PIX,), jnp.float32), jnp.zeros((PIX,), jnp.float32)), splat_list
    )
    return (colour_sum.T, splat_grads)


def on_device(params, first_moment, second_moment, view_basis, target, tile_blocks, moving):
    per_device = params.shape[0]
    projected = project(params, view_basis)
    listed = tile_blocks[0]
    region_blocks = lax.all_gather(projected, "tile", axis=0, tiled=True)
    splat_list = jnp.take(region_blocks, listed, axis=0)
    picture, splat_grads = composite(splat_list, target[0])
    region_count = lax.axis_size("tile") * per_device
    onehot = (listed[:, None] == jnp.arange(region_count)[None, :]).astype(jnp.float32)
    dense_grads = jnp.einsum("lr,lkg->rkg", onehot, splat_grads, precision=highest)
    proj_grads = lax.psum_scatter(dense_grads, "tile", scatter_dimension=0, tiled=True)
    _, pullback = jax.vjp(lambda values: project(values, view_basis), params)
    gradient = pullback(proj_grads)[0]
    rates = step_rates()[:, None]
    moment_one = beta_one * first_moment + (1.0 - beta_one) * gradient
    moment_two = beta_two * second_moment + (1.0 - beta_two) * gradient * gradient
    stepped = params - rates * (moment_one / (1.0 - beta_one**adam_step)) / (
        jnp.sqrt(moment_two / (1.0 - beta_two**adam_step)) + adam_eps
    )
    leaving_ids = moving[0]
    incoming = shifted(
        (
            jnp.take(stepped, leaving_ids, axis=0),
            jnp.take(moment_one, leaving_ids, axis=0),
            jnp.take(moment_two, leaving_ids, axis=0),
        ),
        "region",
        1,
    )
    new_params = stepped.at[leaving_ids].set(incoming[0])
    new_first = moment_one.at[leaving_ids].set(incoming[1])
    new_second = moment_two.at[leaving_ids].set(incoming[2])
    return (new_params, new_first, new_second, picture[None])


def solution(mesh):
    in_specs = (
        P(("region", "tile"), None, None),
        P(("region", "tile"), None, None),
        P(("region", "tile"), None, None),
        P(),
        P(("region", "tile"), None, None),
        P(("region", "tile"), None),
        P(("region", "tile"), None),
    )
    out_specs = (
        P(("region", "tile"), None, None),
        P(("region", "tile"), None, None),
        P(("region", "tile"), None, None),
        P(("region", "tile"), None, None),
    )
    return jax.shard_map(
        on_device, mesh=mesh, in_specs=in_specs, out_specs=out_specs, check_vma=False
    )
```

profile of v0, /device:TPU:0, one launch (start us, length us, event | category | flops | bytes accessed | tf_op | source)
XLA Modules:
  0.0 99.5 jit_solution(8393477302530917290)
XLA Ops:
  11.3 15.2 %all_gather.3 = f32[32,9,128]{2,0,1:T(8,128)S(1)} all-gather(f32[8,9,128]{2,0,1:T(8,128)S(1)} %constant_dynamic-update-slice_fusion), channel_id=1, replica_groups=mesh['region'=8,'tile'=4] {'tile'}, dimensions={0}, use_global_device_ids=true | all-gather | bytes 184320 | tf_op jit(solution)/shard_map/all_gather | solution.py:173
  27.2 9.0 %while.28 = (s32[]{:T(128)}, f32[1024]{0:T(1024)S(1)}, f32[1024,3]{0,1:T(4,128)S(1)}, f32[4,9,128]{2,1,0:T(8,128)S(1)}, s32[]{:T(128)}, /*index=5*/s32[]{:T(128)}, s32[]{}, s32[]{}, s32[]{}, s32[]{}, /*index=10*/s32[]{}, s32[]{}) while((s32[]{:T(128)}, f32[1024]{0:T(1024)S(1)}, f32[1024,3]{0,1:T(4,128)S(1)}, ...), condition=%wide.region_3.4_spmd.clone, body=%wide.region_1.3_spmd.clone.sunk | while | flops 211475584 | bytes 1140968 | solution.py:133
  27.8 1.1 %fusion.161 = f32[1024,128]{1,0:T(8,128)S(1)} fusion(f32[1024]{0:T(1024)S(1)} %get-tuple-element.376, f32[128]{0:T(128)S(1)} %get-tuple-element.367, f32[128]{0:T(128)S(1)} %get-tuple-element.368, f32[1024]{0:T(1024)S(1)} %get-tuple-element.369, f32[128]{0:T(128)S(1)} %get-tuple-element.370, f32[128]{0:T(128)S(1)} %get-tuple-element.371, ...), kind=kOutput, calls=%fused_computation.16.clone.1 | convolution fusion | flops 204898304 | bytes 539648 | tf_op jit(solution)/shard_map/while/body/eval_jaxpr/dot_general | solution.py:127
  30.1 1.1 %fusion.161 = f32[1024,128]{1,0:T(8,128)S(1)} fusion(f32[1024]{0:T(1024)S(1)} %get-tuple-element.376, f32[128]{0:T(128)S(1)} %get-tuple-element.367, f32[128]{0:T(128)S(1)} %get-tuple-element.368, f32[1024]{0:T(1024)S(1)} %get-tuple-element.369, f32[128]{0:T(128)S(1)} %get-tuple-element.370, f32[128]{0:T(128)S(1)} %get-tuple-element.371, ...), kind=kOutput, calls=%fused_computation.16.clone.1 | convolution fusion | flops 204898304 | bytes 539648 | tf_op jit(solution)/shard_map/while/body/eval_jaxpr/dot_general | solution.py:127
  32.3 1.1 %fusion.161 = f32[1024,128]{1,0:T(8,128)S(1)} fusion(f32[1024]{0:T(1024)S(1)} %get-tuple-element.376, f32[128]{0:T(128)S(1)} %get-tuple-element.367, f32[128]{0:T(128)S(1)} %get-tuple-element.368, f32[1024]{0:T(1024)S(1)} %get-tuple-element.369, f32[128]{0:T(128)S(1)} %get-tuple-element.370, f32[128]{0:T(128)S(1)} %get-tuple-element.371, ...), kind=kOutput, calls=%fused_computation.16.clone.1 | convolution fusion | flops 204898304 | bytes 539648 | tf_op jit(solution)/shard_map/while/body/eval_jaxpr/dot_general | solution.py:127
  34.6 1.1 %fusion.161 = f32[1024,128]{1,0:T(8,128)S(1)} fusion(f32[1024]{0:T(1024)S(1)} %get-tuple-element.376, f32[128]{0:T(128)S(1)} %get-tuple-element.367, f32[128]{0:T(128)S(1)} %get-tuple-element.368, f32[1024]{0:T(1024)S(1)} %get-tuple-element.369, f32[128]{0:T(128)S(1)} %get-tuple-element.370, f32[128]{0:T(128)S(1)} %get-tuple-element.371, ...), kind=kOutput, calls=%fused_computation.16.clone.1 | convolution fusion | flops 204898304 | bytes 539648 | tf_op jit(solution)/shard_map/while/body/eval_jaxpr/dot_general | solution.py:127
  36.3 20.6 %while.29 = (s32[]{:T(128)}, f32[1024]{0:T(1024)S(1)}, f32[1024]{0:T(1024)S(1)}, f32[4,9,128]{2,0,1:T(4,128)S(1)}, f32[4,9,128]{2,1,0:T(8,128)S(1)}, /*index=5*/...) while((s32[]{:T(128)}, f32[1024]{0:T(1024)S(1)}, ...), condition=%wide.region_13.14_spmd.clone, body=%wide.region_5.13_spmd.clone.sunk | while | flops 423183744 | bytes 3303176 | solution.py:163
  36.4 1.0 fusion.167
  37.3 1.0 %convolution_bitcast_fusion.4 = f32[1024,128]{1,0:T(8,128)S(1)} fusion(f32[1024,3]{0,1:T(4,128)S(1)} %get-tuple-element.472, f32[4,9,128]{2,1,0:T(8,128)S(1)} %get-tuple-element.471, s32[]{:T(128)} %get-tuple-element.452, s32[]{:T(128)S(6)} %add.964), kind=kOutput, calls=%fused_computation.79.clone.1 | convolution fusion | flops 4718592 | bytes 542728 | tf_op jit(solution)/shard_map/while/body/eval_jaxpr/dot_general | solution.py:143
  38.3 1.8 %fusion.168 = (f32[128]{0:T(128)S(1)}, f32[128]{0:T(128)S(1)}, f32[128]{0:T(128)S(1)}, f32[128]{0:T(128)S(1)}, f32[128]{0:T(128)S(1)}, /*index=5*/f32[128]{0:T(128)S(1)}, f32[1024]{0:T(1024)S(1)}, f32[1024,128]{1,0:T(8,128)S(1)}) fusion(f32[128]{0:T(128)S(1)} %get-tuple-element.384, f32[1024]{0:T(1024)S(1)} %get-tuple-element.385, ...), kind=kOutput, calls=%fused_computation.98.clone.1 | convolution fusion | flops 208828672 | bytes 1600000 | tf_op jit(solution)/shard_map/while/body/eval_jaxpr/dot_general | solution.py:144
  41.5 1.0 fusion.167
  42.5 1.0 %convolution_bitcast_fusion.4 = f32[1024,128]{1,0:T(8,128)S(1)} fusion(f32[1024,3]{0,1:T(4,128)S(1)} %get-tuple-element.472, f32[4,9,128]{2,1,0:T(8,128)S(1)} %get-tuple-element.471, s32[]{:T(128)} %get-tuple-element.452, s32[]{:T(128)S(6)} %add.964), kind=kOutput, calls=%fused_computation.79.clone.1 | convolution fusion | flops 4718592 | bytes 542728 | tf_op jit(solution)/shard_map/while/body/eval_jaxpr/dot_general | solution.py:143
  43.5 1.8 %fusion.168 = (f32[128]{0:T(128)S(1)}, f32[128]{0:T(128)S(1)}, f32[128]{0:T(128)S(1)}, f32[128]{0:T(128)S(1)}, f32[128]{0:T(128)S(1)}, /*index=5*/f32[128]{0:T(128)S(1)}, f32[1024]{0:T(1024)S(1)}, f32[1024,128]{1,0:T(8,128)S(1)}) fusion(f32[128]{0:T(128)S(1)} %get-tuple-element.384, f32[1024]{0:T(1024)S(1)} %get-tuple-element.385, ...), kind=kOutput, calls=%fused_computation.98.clone.1 | convolution fusion | flops 208828672 | bytes 1600000 | tf_op jit(solution)/shard_map/while/body/eval_jaxpr/dot_general | solution.py:144
  46.6 1.0 fusion.167
  47.6 1.0 %convolution_bitcast_fusion.4 = f32[1024,128]{1,0:T(8,128)S(1)} fusion(f32[1024,3]{0,1:T(4,128)S(1)} %get-tuple-element.472, f32[4,9,128]{2,1,0:T(8,128)S(1)} %get-tuple-element.471, s32[]{:T(128)} %get-tuple-element.452, s32[]{:T(128)S(6)} %add.964), kind=kOutput, calls=%fused_computation.79.clone.1 | convolution fusion | flops 4718592 | bytes 542728 | tf_op jit(solution)/shard_map/while/body/eval_jaxpr/dot_general | solution.py:143
  48.6 1.8 %fusion.168 = (f32[128]{0:T(128)S(1)}, f32[128]{0:T(128)S(1)}, f32[128]{0:T(128)S(1)}, f32[128]{0:T(128)S(1)}, f32[128]{0:T(128)S(1)}, /*index=5*/f32[128]{0:T(128)S(1)}, f32[1024]{0:T(1024)S(1)}, f32[1024,128]{1,0:T(8,128)S(1)}) fusion(f32[128]{0:T(128)S(1)} %get-tuple-element.384, f32[1024]{0:T(1024)S(1)} %get-tuple-element.385, ...), kind=kOutput, calls=%fused_computation.98.clone.1 | convolution fusion | flops 208828672 | bytes 1600000 | tf_op jit(solution)/shard_map/while/body/eval_jaxpr/dot_general | solution.py:144
  51.8 1.0 fusion.167
  52.8 1.0 %convolution_bitcast_fusion.4 = f32[1024,128]{1,0:T(8,128)S(1)} fusion(f32[1024,3]{0,1:T(4,128)S(1)} %get-tuple-element.472, f32[4,9,128]{2,1,0:T(8,128)S(1)} %get-tuple-element.471, s32[]{:T(128)} %get-tuple-element.452, s32[]{:T(128)S(6)} %add.964), kind=kOutput, calls=%fused_computation.79.clone.1 | convolution fusion | flops 4718592 | bytes 542728 | tf_op jit(solution)/shard_map/while/body/eval_jaxpr/dot_general | solution.py:143
  53.8 1.8 %fusion.168 = (f32[128]{0:T(128)S(1)}, f32[128]{0:T(128)S(1)}, f32[128]{0:T(128)S(1)}, f32[128]{0:T(128)S(1)}, f32[128]{0:T(128)S(1)}, /*index=5*/f32[128]{0:T(128)S(1)}, f32[1024]{0:T(1024)S(1)}, f32[1024,128]{1,0:T(8,128)S(1)}) fusion(f32[128]{0:T(128)S(1)} %get-tuple-element.384, f32[1024]{0:T(1024)S(1)} %get-tuple-element.385, ...), kind=kOutput, calls=%fused_computation.98.clone.1 | convolution fusion | flops 208828672 | bytes 1600000 | tf_op jit(solution)/shard_map/while/body/eval_jaxpr/dot_general | solution.py:144
  56.9 1.0 %fusion.122 = f32[32,9,128]{2,0,1:T(8,128)} fusion(f32[4,9,128]{2,0,1:T(4,128)S(1)} %get-tuple-element.100, s32[4]{0:T(128)S(1)} %bitcast.135), kind=kOutput, calls=%fused_computation.272 | convolution fusion | flops 1769600 | bytes 165904 | tf_op jit(solution)/shard_map/lr,lkg->rkg/dot_general | solution.py:178
  59.1 19.5 %reduce-scatter.2.cloned.1.call-done = f32[8,9,128]{2,0,1:T(8,128)} async-done(((f32[32,9,128]{2,0,1:T(8,128)}), f32[8,9,128]{2,0,1:T(8,128)}) %reduce-scatter.2.cloned.1.call-update) | async-done | bytes 36880 | tf_op jit(solution)/shard_map/reduce_scatter | solution.py:179
  82.9 1.6 %collective-permute-start.1 = (f32[4,59,128]{2,1,0:T(8,128)S(1)}, f32[4,59,128]{2,1,0:T(8,128)S(1)}, u32[]{:S(2)}, u32[]{:S(2)}) collective-permute-start(f32[4,59,128]{2,1,0:T(8,128)S(1)} %get-tuple-element.274), channel_id=1, source_target_pairs={{0,4},{4,8},{8,12},{12,16},{16,20},{20,24},{24,28},{28,0},{1,5},{5... | collective-permute-start | bytes 362504 | tf_op jit(solution)/shard_map/ppermute | solution.py:18
  84.5 3.6 %collective-permute-done.2 = f32[4,59,128]{2,1,0:T(8,128)S(1)} collective-permute-done((f32[4,59,128]{2,1,0:T(8,128)S(1)}, f32[4,59,128]{2,1,0:T(8,128)S(1)}, u32[]{:S(2)}, u32[]{:S(2)}) %collective-permute-start.2) | collective-permute-done | bytes 120864 | tf_op jit(solution)/shard_map/ppermute | solution.py:18
  88.8 0.8 copy.41
  (140 shorter events, 23.6 us)
Async XLA Ops:
  7.2 3.0 %copy-start = (f32[8,59,128]{2,0,1:T(8,128)S(1)}, f32[8,59,128]{2,0,1:T(8,128)}, u32[]{:S(2)}) copy-start(f32[8,59,128]{2,0,1:T(8,128)} %param.13) | copy-start | bytes 724996
  7.2 71.5 %reduce-scatter.2.cloned.1.call-start = ((), (), s32[]{:S(2)}) async-start(), calls=%async_computation.1 | async-start | bytes 184320 | tf_op jit(solution)/shard_map/reduce_scatter | solution.py:179
  9.4 0.7 copy-start.6
  10.1 0.9 slice-start
  10.3 0.8 copy-start.5
  27.2 9.0 %copy-start.4 = (f32[1,3,1024]{2,0,1:T(1,128)S(1)}, f32[1,3,1024]{2,0,1:T(1,128)}, u32[]{:S(2)}) copy-start(f32[1,3,1024]{2,0,1:T(1,128)} %param.17) | copy-start | bytes 36868
  57.9 0.7 copy-start.8
  78.7 0.8 copy-start.3
  79.6 0.9 copy-start.1
  79.6 1.1 %copy-start.2 = (f32[8,59,128]{2,0,1:T(8,128)S(1)}, f32[8,59,128]{2,0,1:T(8,128)}, u32[]{:S(2)}) copy-start(f32[8,59,128]{2,0,1:T(8,128)} %param.15) | copy-start | bytes 724996
  79.8 0.8 copy-start.7
  82.8 5.3 %collective-permute-start.2 = (f32[4,59,128]{2,1,0:T(8,128)S(1)}, f32[4,59,128]{2,1,0:T(8,128)S(1)}, u32[]{:S(2)}, u32[]{:S(2)}) collective-permute-start(f32[4,59,128]{2,1,0:T(8,128)S(1)} %get-tuple-element.273), channel_id=1, source_target_pairs={{0,4},{4,8},{8,12},{12,16},{16,20},{20,24},{24,28},{28,0},{1,5},{5... | collective-permute-start | bytes 362504 | tf_op jit(solution)/shard_map/ppermute | solution.py:18
  82.9 6.8 %collective-permute-start.1 = (f32[4,59,128]{2,1,0:T(8,128)S(1)}, f32[4,59,128]{2,1,0:T(8,128)S(1)}, u32[]{:S(2)}, u32[]{:S(2)}) collective-permute-start(f32[4,59,128]{2,1,0:T(8,128)S(1)} %get-tuple-element.274), channel_id=1, source_target_pairs={{0,4},{4,8},{8,12},{12,16},{16,20},{20,24},{24,28},{28,0},{1,5},{5... | collective-permute-start | bytes 362504 | tf_op jit(solution)/shard_map/ppermute | solution.py:18
  84.5 6.7 %collective-permute-start = (f32[4,59,128]{2,1,0:T(8,128)S(1)}, f32[4,59,128]{2,1,0:T(8,128)S(1)}, u32[]{:S(2)}, u32[]{:S(2)}) collective-permute-start(f32[4,59,128]{2,1,0:T(8,128)S(1)} %get-tuple-element.275), channel_id=1, source_target_pairs={{0,4},{4,8},{8,12},{12,16},{16,20},{20,24},{24,28},{28,0},{1,5},{5... | collective-permute-start | bytes 362504 | tf_op jit(solution)/shard_map/ppermute | solution.py:18
Sparse Core Ops, SparseCore 0:
  58.0 20.6 reduce-scatter.1
where the time goes:
time: 99.8 us; the launch traced here: 99.5 us
  matrix products  25.5 us (26%)
  waiting for transfers between devices  23.2 us (23%)
  blocking collectives  15.2 us (15%)
  between operations  14.4 us (14%)
  local copies, waits for them, and re-layouts  12.6 us (13%)
  other arithmetic  6.27 us (6%)
  starting transfers between devices  1.75 us (2%)
    reduce_scatter x1, waiting for transfers between devices, on_device(): lax.psum_scatter(dense_grads, 'tile', scatter_dimension=0, tiled=True)  19.5 us
    all_gather x1, blocking collectives, on_device(): region_blocks = lax.all_gather(projected, 'tile', axis=0, tiled=True)  15.2 us
    dot_general x4, matrix products, backward(): jnp.dot(weight * shading, inclusive_mask, precision=highest)  7.1 us
    unnamed x21, local copies, waits for them, and re-layouts  4.67 us
    dot_general x4, matrix products, forward(): log_here = log_trans[:, None] + jnp.dot(log_keep, strict, precision=highest)  4.21 us
    dot_general x4, matrix products, backward(): shading = jnp.dot(errors, splats[6:9], precision=highest)  4.01 us
    dot_general x4, matrix products, backward(): log_here = log_trans[:, None] + jnp.dot(log_keep, strict, precision=highest)  3.89 us
    ppermute x3, waiting for transfers between devices, shifted(): lax.ppermute(shard, axis, [(i, (i + by) % peers) for i in range(peers)])  3.62 us
  transfers between devices with their start and end apart: 4, of which 2 were waited for; matrix products, arithmetic and copies ran while one was open for 4% of the time, Pallas kernels for 0%

commit v1 on v0

--- a/solution.py
+++ b/solution.py
@@ -170,7 +170,18 @@
     per_device = params.shape[0]
     projected = project(params, view_basis)
     listed = tile_blocks[0]
-    region_blocks = lax.all_gather(projected, "tile", axis=0, tiled=True)
+    ways = lax.axis_size("tile")
+    up = [(d, (d + 1) % ways) for d in range(ways)]
+    down = [(d, (d - 1) % ways) for d in range(ways)]
+    earlier, later = ([projected], [projected])
+    for __2 in range(ways // 2):
+        earlier.append(lax.ppermute(earlier[-1], "tile", up))
+    for __2 in range((ways - 1) // 2):
+        later.append(lax.ppermute(later[-1], "tile", down))
+    line = jnp.concatenate([*earlier[::-1], *later[1:]], axis=0)
+    region_blocks = jnp.roll(
+        line, (lax.axis_index("tile") - ways // 2) * projected.shape[0], axis=0
+    )
     splat_list = jnp.take(region_blocks, listed, axis=0)
     picture, splat_grads = composite(splat_list, target[0])
     region_count = lax.axis_size("tile") * per_device

time: 99.8 us -> 94.3 us (0.945)
  blocking collectives: 15.2 us -> 0 us
  starting transfers between devices: 1.75 us -> 6.89 us
  waiting for transfers between devices: 23.2 us -> 27.9 us
    all_gather x1 -> x0, blocking collectives: 15.2 us -> none  [on_device(): region_blocks = lax.all_gather(projected, 'tile', axis=0, tiled=True)]
    ppermute x0 -> x3, waiting for transfers between devices: none -> 6.98 us  [the longest x2 6.98 us: on_device(): earlier.append(lax.ppermute(earlier[-1], 'tile', up))]
    ppermute x0 -> x3, starting transfers between devices: none -> 5.17 us  [the longest x2 3.08 us: on_device(): earlier.append(lax.ppermute(earlier[-1], 'tile', up))]
    reduce_scatter x1, waiting for transfers between devices: 19.5 us -> 17.8 us  [on_device(): lax.psum_scatter(dense_grads, 'tile', scatter_dimension=0, tiled=True)]
    unnamed x21 -> x30, local copies, waits for them, and re-layouts: 4.67 us -> 4.07 us
  transfers between devices with their start and end apart: 4 -> 7, of which waited for: 2 -> 4; matrix products, arithmetic and copies ran while one was open for 4% -> 4% of each run, Pallas kernels for 0% -> 0%
where the time goes in v1:
time: 94.3 us; the launch traced here: 93.9 us
  waiting for transfers between devices  27.9 us (30%)
  matrix products  25.5 us (27%)
  between operations  14.6 us (15%)
  local copies, waits for them, and re-layouts  12.1 us (13%)
  starting transfers between devices  6.89 us (7%)
  other arithmetic  6.35 us (7%)
    reduce_scatter x1, waiting for transfers between devices, on_device(): lax.psum_scatter(dense_grads, 'tile', scatter_dimension=0, tiled=True)  17.8 us
    dot_general x4, matrix products, backward(): jnp.dot(weight * shading, inclusive_mask, precision=highest)  7.07 us
    ppermute x2, waiting for transfers between devices, on_device(): earlier.append(lax.ppermute(earlier[-1], 'tile', up))  6.98 us
    dot_general x4, matrix products, forward(): log_here = log_trans[:, None] + jnp.dot(log_keep, strict, precision=highest)  4.22 us
    unnamed x30, local copies, waits for them, and re-layouts  4.07 us
    dot_general x4, matrix products, backward(): shading = jnp.dot(errors, splats[6:9], precision=highest)  4.01 us
    dot_general x4, matrix products, backward(): log_here = log_trans[:, None] + jnp.dot(log_keep, strict, precision=highest)  3.9 us
    ppermute x2, starting transfers between devices, on_device(): earlier.append(lax.ppermute(earlier[-1], 'tile', up))  3.08 us
  transfers between devices with their start and end apart: 7, of which 4 were waited for; matrix products, arithmetic and copies ran while one was open for 4% of the time, Pallas kernels for 0%

profile of v1, /device:TPU:0, one launch (start us, length us, event | category | flops | bytes accessed | tf_op | source)
XLA Modules:
  0.0 93.9 jit_solution(9626013619740349690)
XLA Ops:
  10.6 3.1 %collective-permute-start = (f32[8,9,128]{2,0,1:T(8,128)S(1)}, f32[8,9,128]{2,0,1:T(8,128)S(1)}, u32[]{:S(2)}, u32[]{:S(2)}) collective-permute-start(f32[8,9,128]{2,0,1:T(8,128)S(1)} %constant_dynamic-update-slice_fusion), channel_id=1, source_target_pairs={{0,1},{1,2},{2,3},{3,0},{4,5},{5,6},{6,7},{7,4},{8,9},{9,10},{10,1... | collective-permute-start | bytes 110600 | tf_op jit(solution)/shard_map/ppermute | solution.py:178
  13.7 2.1 %collective-permute-start.2 = (f32[8,9,128]{2,0,1:T(8,128)S(1)}, f32[8,9,128]{2,0,1:T(8,128)S(1)}, u32[]{:S(2)}, u32[]{:S(2)}) collective-permute-start(f32[8,9,128]{2,0,1:T(8,128)S(1)} %constant_dynamic-update-slice_fusion), channel_id=1, source_target_pairs={{0,3},{1,0},{2,1},{3,2},{4,7},{5,4},{6,5},{7,6},{8,11},{9,8},{10,9... | collective-permute-start | bytes 110600 | tf_op jit(solution)/shard_map/ppermute | solution.py:180
  16.5 1.3 %collective-permute-done = f32[8,9,128]{2,0,1:T(8,128)S(1)} collective-permute-done((f32[8,9,128]{2,0,1:T(8,128)S(1)}, f32[8,9,128]{2,0,1:T(8,128)S(1)}, u32[]{:S(2)}, u32[]{:S(2)}) %collective-permute-start) | collective-permute-done | bytes 36896 | tf_op jit(solution)/shard_map/ppermute | solution.py:178
  17.9 5.7 %collective-permute-done.1 = f32[8,9,128]{2,0,1:T(8,128)S(1)} collective-permute-done((f32[8,9,128]{2,0,1:T(8,128)S(1)}, f32[8,9,128]{2,0,1:T(8,128)S(1)}, u32[]{:S(2)}, u32[]{:S(2)}) %collective-permute-start.1) | collective-permute-done | bytes 36896 | tf_op jit(solution)/shard_map/ppermute | solution.py:178
  24.6 9.0 %while.28 = (s32[]{:T(128)}, f32[1024]{0:T(1024)S(1)}, f32[1024,3]{0,1:T(4,128)S(1)}, f32[4,9,128]{2,1,0:T(8,128)S(1)}, s32[]{:T(128)}, /*index=5*/s32[]{:T(128)}, s32[]{}, s32[]{}, s32[]{}, s32[]{}, /*index=10*/s32[]{}, s32[]{}) while((s32[]{:T(128)}, f32[1024]{0:T(1024)S(1)}, f32[1024,3]{0,1:T(4,128)S(1)}, ...), condition=%wide.region_3.4_spmd.clone, body=%wide.region_1.3_spmd.clone.sunk | while | flops 211475584 | bytes 1140968 | solution.py:133
  25.2 1.1 %fusion.161 = f32[1024,128]{1,0:T(8,128)S(1)} fusion(f32[1024]{0:T(1024)S(1)} %get-tuple-element.379, f32[128]{0:T(128)S(1)} %get-tuple-element.370, f32[128]{0:T(128)S(1)} %get-tuple-element.371, f32[1024]{0:T(1024)S(1)} %get-tuple-element.372, f32[128]{0:T(128)S(1)} %get-tuple-element.373, f32[128]{0:T(128)S(1)} %get-tuple-element.374, ...), kind=kOutput, calls=%fused_computation.16.clone.1 | convolution fusion | flops 204898304 | bytes 539648 | tf_op jit(solution)/shard_map/while/body/eval_jaxpr/dot_general | solution.py:127
  27.5 1.1 %fusion.161 = f32[1024,128]{1,0:T(8,128)S(1)} fusion(f32[1024]{0:T(1024)S(1)} %get-tuple-element.379, f32[128]{0:T(128)S(1)} %get-tuple-element.370, f32[128]{0:T(128)S(1)} %get-tuple-element.371, f32[1024]{0:T(1024)S(1)} %get-tuple-element.372, f32[128]{0:T(128)S(1)} %get-tuple-element.373, f32[128]{0:T(128)S(1)} %get-tuple-element.374, ...), kind=kOutput, calls=%fused_computation.16.clone.1 | convolution fusion | flops 204898304 | bytes 539648 | tf_op jit(solution)/shard_map/while/body/eval_jaxpr/dot_general | solution.py:127
  29.7 1.1 %fusion.161 = f32[1024,128]{1,0:T(8,128)S(1)} fusion(f32[1024]{0:T(1024)S(1)} %get-tuple-element.379, f32[128]{0:T(128)S(1)} %get-tuple-element.370, f32[128]{0:T(128)S(1)} %get-tuple-element.371, f32[1024]{0:T(1024)S(1)} %get-tuple-element.372, f32[128]{0:T(128)S(1)} %get-tuple-element.373, f32[128]{0:T(128)S(1)} %get-tuple-element.374, ...), kind=kOutput, calls=%fused_computation.16.clone.1 | convolution fusion | flops 204898304 | bytes 539648 | tf_op jit(solution)/shard_map/while/body/eval_jaxpr/dot_general | solution.py:127
  32.0 1.1 %fusion.161 = f32[1024,128]{1,0:T(8,128)S(1)} fusion(f32[1024]{0:T(1024)S(1)} %get-tuple-element.379, f32[128]{0:T(128)S(1)} %get-tuple-element.370, f32[128]{0:T(128)S(1)} %get-tuple-element.371, f32[1024]{0:T(1024)S(1)} %get-tuple-element.372, f32[128]{0:T(128)S(1)} %get-tuple-element.373, f32[128]{0:T(128)S(1)} %get-tuple-element.374, ...), kind=kOutput, calls=%fused_computation.16.clone.1 | convolution fusion | flops 204898304 | bytes 539648 | tf_op jit(solution)/shard_map/while/body/eval_jaxpr/dot_general | solution.py:127
  33.7 20.5 %while.29 = (s32[]{:T(128)}, f32[1024]{0:T(1024)S(1)}, f32[1024]{0:T(1024)S(1)}, f32[4,9,128]{2,0,1:T(4,128)S(1)}, f32[4,9,128]{2,1,0:T(8,128)S(1)}, /*index=5*/...) while((s32[]{:T(128)}, f32[1024]{0:T(1024)S(1)}, ...), condition=%wide.region_13.14_spmd.clone, body=%wide.region_5.13_spmd.clone.sunk | while | flops 423183744 | bytes 3303176 | solution.py:163
  34.7 1.0 %convolution_bitcast_fusion.4 = f32[1024,128]{1,0:T(8,128)S(1)} fusion(f32[1024,3]{0,1:T(4,128)S(1)} %get-tuple-element.475, f32[4,9,128]{2,1,0:T(8,128)S(1)} %get-tuple-element.474, s32[]{:T(128)} %get-tuple-element.455, s32[]{:T(128)S(6)} %add.997), kind=kOutput, calls=%fused_computation.79.clone.1 | convolution fusion | flops 4718592 | bytes 542728 | tf_op jit(solution)/shard_map/while/body/eval_jaxpr/dot_general | solution.py:143
  35.7 1.8 %fusion.168 = (f32[128]{0:T(128)S(1)}, f32[128]{0:T(128)S(1)}, f32[128]{0:T(128)S(1)}, f32[128]{0:T(128)S(1)}, f32[128]{0:T(128)S(1)}, /*index=5*/f32[128]{0:T(128)S(1)}, f32[1024]{0:T(1024)S(1)}, f32[1024,128]{1,0:T(8,128)S(1)}) fusion(f32[128]{0:T(128)S(1)} %get-tuple-element.387, f32[1024]{0:T(1024)S(1)} %get-tuple-element.388, ...), kind=kOutput, calls=%fused_computation.98.clone.1 | convolution fusion | flops 208828672 | bytes 1600000 | tf_op jit(solution)/shard_map/while/body/eval_jaxpr/dot_general | solution.py:144
  38.9 1.0 %fusion.167 = f32[1024,128]{1,0:T(8,128)S(1)} fusion(f32[1024]{0:T(1024)S(1)} %broadcast_select_fusion.8, f32[128]{0:T(128)S(1)} %get-tuple-element.389, f32[128]{0:T(128)S(1)} %get-tuple-element.387, f32[1024]{0:T(1024)S(1)} %get-tuple-element.388, f32[128]{0:T(128)S(1)} %get-tuple-element.390, f32[128]{0:T(128)S(1)} %get-tuple-element.391, ...), kind=kOutput, calls=%fused_computation.81.clone.1 | convolution fusion | flops 203194368 | bytes 539648 | tf_op jit(solution)/shard_map/while/body/eval_jaxpr/dot_general | solution.py:140
  39.9 1.0 %convolution_bitcast_fusion.4 = f32[1024,128]{1,0:T(8,128)S(1)} fusion(f32[1024,3]{0,1:T(4,128)S(1)} %get-tuple-element.475, f32[4,9,128]{2,1,0:T(8,128)S(1)} %get-tuple-element.474, s32[]{:T(128)} %get-tuple-element.455, s32[]{:T(128)S(6)} %add.997), kind=kOutput, calls=%fused_computation.79.clone.1 | convolution fusion | flops 4718592 | bytes 542728 | tf_op jit(solution)/shard_map/while/body/eval_jaxpr/dot_general | solution.py:143
  40.9 1.8 %fusion.168 = (f32[128]{0:T(128)S(1)}, f32[128]{0:T(128)S(1)}, f32[128]{0:T(128)S(1)}, f32[128]{0:T(128)S(1)}, f32[128]{0:T(128)S(1)}, /*index=5*/f32[128]{0:T(128)S(1)}, f32[1024]{0:T(1024)S(1)}, f32[1024,128]{1,0:T(8,128)S(1)}) fusion(f32[128]{0:T(128)S(1)} %get-tuple-element.387, f32[1024]{0:T(1024)S(1)} %get-tuple-element.388, ...), kind=kOutput, calls=%fused_computation.98.clone.1 | convolution fusion | flops 208828672 | bytes 1600000 | tf_op jit(solution)/shard_map/while/body/eval_jaxpr/dot_general | solution.py:144
  44.0 1.0 %fusion.167 = f32[1024,128]{1,0:T(8,128)S(1)} fusion(f32[1024]{0:T(1024)S(1)} %broadcast_select_fusion.8, f32[128]{0:T(128)S(1)} %get-tuple-element.389, f32[128]{0:T(128)S(1)} %get-tuple-element.387, f32[1024]{0:T(1024)S(1)} %get-tuple-element.388, f32[128]{0:T(128)S(1)} %get-tuple-element.390, f32[128]{0:T(128)S(1)} %get-tuple-element.391, ...), kind=kOutput, calls=%fused_computation.81.clone.1 | convolution fusion | flops 203194368 | bytes 539648 | tf_op jit(solution)/shard_map/while/body/eval_jaxpr/dot_general | solution.py:140
  45.0 1.0 %convolution_bitcast_fusion.4 = f32[1024,128]{1,0:T(8,128)S(1)} fusion(f32[1024,3]{0,1:T(4,128)S(1)} %get-tuple-element.475, f32[4,9,128]{2,1,0:T(8,128)S(1)} %get-tuple-element.474, s32[]{:T(128)} %get-tuple-element.455, s32[]{:T(128)S(6)} %add.997), kind=kOutput, calls=%fused_computation.79.clone.1 | convolution fusion | flops 4718592 | bytes 542728 | tf_op jit(solution)/shard_map/while/body/eval_jaxpr/dot_general | solution.py:143
  46.0 1.8 %fusion.168 = (f32[128]{0:T(128)S(1)}, f32[128]{0:T(128)S(1)}, f32[128]{0:T(128)S(1)}, f32[128]{0:T(128)S(1)}, f32[128]{0:T(128)S(1)}, /*index=5*/f32[128]{0:T(128)S(1)}, f32[1024]{0:T(1024)S(1)}, f32[1024,128]{1,0:T(8,128)S(1)}) fusion(f32[128]{0:T(128)S(1)} %get-tuple-element.387, f32[1024]{0:T(1024)S(1)} %get-tuple-element.388, ...), kind=kOutput, calls=%fused_computation.98.clone.1 | convolution fusion | flops 208828672 | bytes 1600000 | tf_op jit(solution)/shard_map/while/body/eval_jaxpr/dot_general | solution.py:144
  50.1 1.0 %convolution_bitcast_fusion.4 = f32[1024,128]{1,0:T(8,128)S(1)} fusion(f32[1024,3]{0,1:T(4,128)S(1)} %get-tuple-element.475, f32[4,9,128]{2,1,0:T(8,128)S(1)} %get-tuple-element.474, s32[]{:T(128)} %get-tuple-element.455, s32[]{:T(128)S(6)} %add.997), kind=kOutput, calls=%fused_computation.79.clone.1 | convolution fusion | flops 4718592 | bytes 542728 | tf_op jit(solution)/shard_map/while/body/eval_jaxpr/dot_general | solution.py:143
  51.1 1.8 %fusion.168 = (f32[128]{0:T(128)S(1)}, f32[128]{0:T(128)S(1)}, f32[128]{0:T(128)S(1)}, f32[128]{0:T(128)S(1)}, f32[128]{0:T(128)S(1)}, /*index=5*/f32[128]{0:T(128)S(1)}, f32[1024]{0:T(1024)S(1)}, f32[1024,128]{1,0:T(8,128)S(1)}) fusion(f32[128]{0:T(128)S(1)} %get-tuple-element.387, f32[1024]{0:T(1024)S(1)} %get-tuple-element.388, ...), kind=kOutput, calls=%fused_computation.98.clone.1 | convolution fusion | flops 208828672 | bytes 1600000 | tf_op jit(solution)/shard_map/while/body/eval_jaxpr/dot_general | solution.py:144
  54.2 1.0 %fusion.122 = f32[32,9,128]{2,0,1:T(8,128)} fusion(f32[4,9,128]{2,0,1:T(4,128)S(1)} %get-tuple-element.100, s32[4]{0:T(128)S(1)} %bitcast.139), kind=kOutput, calls=%fused_computation.295 | convolution fusion | flops 1769600 | bytes 165904 | tf_op jit(solution)/shard_map/lr,lkg->rkg/dot_general | solution.py:189
  55.3 17.8 %reduce-scatter.2.cloned.1.call-done = f32[8,9,128]{2,0,1:T(8,128)} async-done(((f32[32,9,128]{2,0,1:T(8,128)}), f32[8,9,128]{2,0,1:T(8,128)}) %reduce-scatter.2.cloned.1.call-update) | async-done | bytes 36880 | tf_op jit(solution)/shard_map/reduce_scatter | solution.py:190
  77.3 1.6 %collective-permute-start.4 = (f32[4,59,128]{2,1,0:T(8,128)S(1)}, f32[4,59,128]{2,1,0:T(8,128)S(1)}, u32[]{:S(2)}, u32[]{:S(2)}) collective-permute-start(f32[4,59,128]{2,1,0:T(8,128)S(1)} %get-tuple-element.277), channel_id=1, source_target_pairs={{0,4},{4,8},{8,12},{12,16},{16,20},{20,24},{24,28},{28,0},{1,5},{5... | collective-permute-start | bytes 362504 | tf_op jit(solution)/shard_map/ppermute | solution.py:18
  79.6 3.0 %collective-permute-done.5 = f32[4,59,128]{2,1,0:T(8,128)S(1)} collective-permute-done((f32[4,59,128]{2,1,0:T(8,128)S(1)}, f32[4,59,128]{2,1,0:T(8,128)S(1)}, u32[]{:S(2)}, u32[]{:S(2)}) %collective-permute-start.5) | collective-permute-done | bytes 120864 | tf_op jit(solution)/shard_map/ppermute | solution.py:18
  (166 shorter events, 25.9 us)
Async XLA Ops:
  7.2 2.3 %copy-start = (f32[8,59,128]{2,0,1:T(8,128)S(1)}, f32[8,59,128]{2,0,1:T(8,128)}, u32[]{:S(2)}) copy-start(f32[8,59,128]{2,0,1:T(8,128)} %param.13) | copy-start | bytes 724996
  7.2 65.9 %reduce-scatter.2.cloned.1.call-start = ((), (), s32[]{:S(2)}) async-start(), calls=%async_computation.1 | async-start | bytes 184320 | tf_op jit(solution)/shard_map/reduce_scatter | solution.py:190
  9.4 0.9 slice-start
  9.5 0.8 copy-start.5
  10.6 5.2 %copy-start.6 = (s32[1,4]{1,0:T(1,128)S(1)}, s32[1,4]{1,0:T(1,128)}, u32[]{:S(2)}) copy-start(s32[1,4]{1,0:T(1,128)} %param.18) | copy-start | bytes 52
  10.6 7.1 %collective-permute-start = (f32[8,9,128]{2,0,1:T(8,128)S(1)}, f32[8,9,128]{2,0,1:T(8,128)S(1)}, u32[]{:S(2)}, u32[]{:S(2)}) collective-permute-start(f32[8,9,128]{2,0,1:T(8,128)S(1)} %constant_dynamic-update-slice_fusion), channel_id=1, source_target_pairs={{0,1},{1,2},{2,3},{3,0},{4,5},{5,6},{6,7},{7,4},{8,9},{9,10},{10,1... | collective-permute-start | bytes 110600 | tf_op jit(solution)/shard_map/ppermute | solution.py:178
  13.7 9.9 %collective-permute-start.2 = (f32[8,9,128]{2,0,1:T(8,128)S(1)}, f32[8,9,128]{2,0,1:T(8,128)S(1)}, u32[]{:S(2)}, u32[]{:S(2)}) collective-permute-start(f32[8,9,128]{2,0,1:T(8,128)S(1)} %constant_dynamic-update-slice_fusion), channel_id=1, source_target_pairs={{0,3},{1,0},{2,1},{3,2},{4,7},{5,4},{6,5},{7,6},{8,11},{9,8},{10,9... | collective-permute-start | bytes 110600 | tf_op jit(solution)/shard_map/ppermute | solution.py:180
  15.8 0.7 copy-start.8
  17.8 5.8 %collective-permute-start.1 = (f32[8,9,128]{2,0,1:T(8,128)S(1)}, f32[8,9,128]{2,0,1:T(8,128)S(1)}, u32[]{:S(2)}, u32[]{:S(2)}) collective-permute-start(f32[8,9,128]{2,0,1:T(8,128)S(1)} %collective-permute-done), channel_id=1, source_target_pairs={{0,1},{1,2},{2,3},{3,0},{4,5},{5,6},{6,7},{7,4},{8,9},{9,10},{10,1... | collective-permute-start | bytes 110600 | tf_op jit(solution)/shard_map/ppermute | solution.py:178
  24.6 9.1 %copy-start.4 = (f32[1,3,1024]{2,0,1:T(1,128)S(1)}, f32[1,3,1024]{2,0,1:T(1,128)}, u32[]{:S(2)}) copy-start(f32[1,3,1024]{2,0,1:T(1,128)} %param.17) | copy-start | bytes 36868
  73.1 0.8 copy-start.3
  74.0 0.9 %copy-start.1 = (f32[8,59,128]{2,0,1:T(8,128)S(1)}, f32[8,59,128]{2,0,1:T(8,128)}, u32[]{:S(2)}) copy-start(f32[8,59,128]{2,0,1:T(8,128)} %param.14) | copy-start | bytes 724996
  74.0 1.1 %copy-start.2 = (f32[8,59,128]{2,0,1:T(8,128)S(1)}, f32[8,59,128]{2,0,1:T(8,128)}, u32[]{:S(2)}) copy-start(f32[8,59,128]{2,0,1:T(8,128)} %param.15) | copy-start | bytes 724996
  74.3 0.8 copy-start.7
  77.2 5.3 %collective-permute-start.5 = (f32[4,59,128]{2,1,0:T(8,128)S(1)}, f32[4,59,128]{2,1,0:T(8,128)S(1)}, u32[]{:S(2)}, u32[]{:S(2)}) collective-permute-start(f32[4,59,128]{2,1,0:T(8,128)S(1)} %get-tuple-element.276), channel_id=1, source_target_pairs={{0,4},{4,8},{8,12},{12,16},{16,20},{20,24},{24,28},{28,0},{1,5},{5... | collective-permute-start | bytes 362504 | tf_op jit(solution)/shard_map/ppermute | solution.py:18
  77.3 6.8 %collective-permute-start.4 = (f32[4,59,128]{2,1,0:T(8,128)S(1)}, f32[4,59,128]{2,1,0:T(8,128)S(1)}, u32[]{:S(2)}, u32[]{:S(2)}) collective-permute-start(f32[4,59,128]{2,1,0:T(8,128)S(1)} %get-tuple-element.277), channel_id=1, source_target_pairs={{0,4},{4,8},{8,12},{12,16},{16,20},{20,24},{24,28},{28,0},{1,5},{5... | collective-permute-start | bytes 362504 | tf_op jit(solution)/shard_map/ppermute | solution.py:18
  78.9 6.7 %collective-permute-start.3 = (f32[4,59,128]{2,1,0:T(8,128)S(1)}, f32[4,59,128]{2,1,0:T(8,128)S(1)}, u32[]{:S(2)}, u32[]{:S(2)}) collective-permute-start(f32[4,59,128]{2,1,0:T(8,128)S(1)} %get-tuple-element.278), channel_id=1, source_target_pairs={{0,4},{4,8},{8,12},{12,16},{16,20},{20,24},{24,28},{28,0},{1,5},{5... | collective-permute-start | bytes 362504 | tf_op jit(solution)/shard_map/ppermute | solution.py:18
Sparse Core Ops, SparseCore 0:
  55.4 17.6 reduce-scatter.1
